TPU v7x, 128 devices: a whole 4x4x4 slice. The times are simulated.
128 devices in a mesh: row: 8 (over z, y_hi), col: 16 (over y_lo, x, core).
Axes of the slice: x: 4, y: 4 (y_hi: 2, y_lo: 2; y = y_hi * 2 + y_lo), z: 4, core: 2. Of those that a mesh axis runs over, the one named last changes fastest.
Arguments:
- object_field: float32 [2, 2, 2048, 4096], P(None, None, 'row', 'col'), may hold values from -0.6 to 1
- probe_modes: float32 [2, 2, 256, 256], replicated, may hold values from -5 to 5
- amplitudes: float32 [2, 24, 16, 256, 256], P(None, 'row', 'col'), may hold values from 0 to 2
- offsets: int32 [2, 2, 24, 16], P(None, None, 'row', 'col'), may hold values from 0 to 255
- counts: int32 [2, 8, 16], P(None, 'row', 'col'), may hold values from 1 to 3, as said below
Outputs:
- new_object: float32 [2, 2, 2048, 4096], P(None, None, 'row', 'col')
- new_probe: float32 [2, 2, 256, 256], replicated
Inputs may be any that keep to these rules, and one draw needn't show every extreme that they name: offsets[b, 0, r * 3 + s, c] and offsets[b, 1, r * 3 + s, c] are the row and column, counted from tile (r, c)'s first cell, of the centre of slot s's 256 x 256 patch in batch b. Tile (r, c) has counts[b, r, c] scan positions in batch b, in its first slots; the other slots are unused; in each batch some tile has 3.
All inputs are finite; a program needn't handle non-finite values.
Results may differ from a plain program's by a relative error of at most 0.02.
Values sent between devices are 32-bit elements; how exact they have to be, the bound alone decides.
A program may use at most 128 MiB of HBM per device.

v0:
```python
import math
import jax
import jax.numpy as jnp
from jax import lax
from jax.sharding import PartitionSpec as P

AMPLITUDE_FLOOR = 0.5
OBJECT_STEP = 0.25
PROBE_STEP = 0.125


def from_behind(value, axis, steps):
    count = lax.axis_size(axis)
    leading, last = (max(0, -steps), min(count, count - steps))
    return lax.ppermute(value, axis, [(source, source + steps) for source in range(leading, last)])


def with_halo(array, sides, width):
    for axis, dim in sides:
        count, length = (lax.axis_size(axis), array.shape[dim])
        up = [(i, (i + 1) % count) for i in range(count - 1)]
        down = [(j, i) for i, j in up]
        last = lax.slice_in_dim(array, length - width, length, axis=dim)
        leading = lax.slice_in_dim(array, 0, width, axis=dim)
        before = lax.ppermute(last, axis, up)
        after = lax.ppermute(leading, axis, down)
        array = jnp.concatenate([before, array, after], axis=dim)
    return array


def tables(pattern_side):
    indices = jnp.arange(pattern_side, dtype=jnp.int32)
    products = indices[:, None] * indices[None, :] % pattern_side
    angles = products.astype(jnp.float32) * (2.0 * math.pi / pattern_side)
    norm_scale = 1.0 / math.sqrt(pattern_side)
    forward_re = (jnp.cos(angles) * norm_scale).astype(jnp.bfloat16)
    forward_im = (-jnp.sin(angles) * norm_scale).astype(jnp.bfloat16)
    frequency = jnp.where(indices < pattern_side // 2, indices, indices - pattern_side)
    phases = (frequency[:, None] * frequency[:, None] + frequency[None, :] * frequency[None, :]) % (
        16 * pattern_side
    )
    chirp_angles = phases.astype(jnp.float32) * (2.0 * math.pi / (16 * pattern_side))
    return (forward_re, forward_im, jnp.cos(chirp_angles), -jnp.sin(chirp_angles))


def contract(form, left, right):
    return jnp.einsum(form, left, right, preferred_element_type=jnp.float32)


def transform(field_re, field_im, table_re, table_im, inverse):
    sign_value = -1.0 if inverse else 1.0
    left_re = field_re.astype(jnp.bfloat16)
    left_im = field_im.astype(jnp.bfloat16)
    first_rr = contract("mjk,kl->mjl", left_re, table_re)
    first_ri = contract("mjk,kl->mjl", left_re, table_im)
    first_ir = contract("mjk,kl->mjl", left_im, table_re)
    first_ii = contract("mjk,kl->mjl", left_im, table_im)
    middle_re = (first_rr - sign_value * first_ii).astype(jnp.bfloat16)
    middle_im = (first_ir + sign_value * first_ri).astype(jnp.bfloat16)
    out_re = contract("jk,mkl->mjl", table_re, middle_re) - sign_value * contract(
        "jk,mkl->mjl", table_im, middle_im
    )
    out_im = contract("jk,mkl->mjl", table_re, middle_im) + sign_value * contract(
        "jk,mkl->mjl", table_im, middle_re
    )
    return (out_re, out_im)


def position_terms(patch_cells, probe_modes, amplitude, dft_table):
    forward_re, forward_im, chirp_re, chirp_im = dft_table
    slice_count = patch_cells.shape[1]
    wave_re = probe_modes[0]
    wave_im = probe_modes[1]
    incoming = []
    for slice_index in range(slice_count):
        incoming.append((wave_re, wave_im))
        object_re = patch_cells[0, slice_index]
        object_im = patch_cells[1, slice_index]
        exit_re = wave_re * object_re - wave_im * object_im
        exit_im = wave_re * object_im + wave_im * object_re
        if slice_index + 1 < slice_count:
            spread_re, spread_im = transform(exit_re, exit_im, forward_re, forward_im, False)
            turned_re = spread_re * chirp_re - spread_im * chirp_im
            turned_im = spread_re * chirp_im + spread_im * chirp_re
            wave_re, wave_im = transform(turned_re, turned_im, forward_re, forward_im, True)
    far_re, far_im = transform(exit_re, exit_im, forward_re, forward_im, False)
    intensity = jnp.sum(far_re * far_re + far_im * far_im, axis=0)
    modulus_ratio = 1.0 - amplitude / jnp.maximum(jnp.sqrt(intensity), AMPLITUDE_FLOOR)
    back_re, back_im = transform(
        far_re * modulus_ratio, far_im * modulus_ratio, forward_re, forward_im, True
    )
    object_terms = [None] * slice_count
    for slice_index in reversed(range(slice_count)):
        wave_re, wave_im = incoming[slice_index]
        object_re = patch_cells[0, slice_index]
        object_im = patch_cells[1, slice_index]
        term_re = jnp.sum(wave_re * back_re + wave_im * back_im, axis=0)
        term_im = jnp.sum(wave_re * back_im - wave_im * back_re, axis=0)
        object_terms[slice_index] = (term_re, term_im)
        inner_re = object_re * back_re + object_im * back_im
        inner_im = object_re * back_im - object_im * back_re
        if slice_index > 0:
            spread_re, spread_im = transform(inner_re, inner_im, forward_re, forward_im, False)
            turned_re = spread_re * chirp_re + spread_im * chirp_im
            turned_im = spread_im * chirp_re - spread_re * chirp_im
            back_re, back_im = transform(turned_re, turned_im, forward_re, forward_im, True)
    object_stack = jnp.stack(
        [
            jnp.stack([pair_terms[0] for pair_terms in object_terms]),
            jnp.stack([pair_terms[1] for pair_terms in object_terms]),
        ]
    )
    probe_stack = jnp.stack([inner_re, inner_im])
    return (object_stack, probe_stack)


def column_strip(piece, offset):
    return from_behind(piece, "col", offset)


def row_strip(piece, offset):
    return from_behind(piece, "row", offset)


def return_sectioned(gradient, rim_width, tile_cells):
    rim_start = rim_width + tile_cells
    rim_end = tile_cells - rim_width
    from_left = column_strip(gradient[:, :, :, rim_start:], 1)
    from_right = column_strip(gradient[:, :, :, :rim_width], -1)
    middle = gradient[:, :, :, rim_width:rim_start]
    middle = middle.at[:, :, :, :rim_width].add(from_left)
    middle = middle.at[:, :, :, rim_end:].add(from_right)
    from_above = row_strip(middle[:, :, rim_start:, :], 1)
    from_below = row_strip(middle[:, :, :rim_width, :], -1)
    tile_grad = middle[:, :, rim_width:rim_start, :]
    tile_grad = tile_grad.at[:, :, :rim_width, :].add(from_above)
    tile_grad = tile_grad.at[:, :, rim_end:, :].add(from_below)
    return tile_grad


def body(object_field, probe_modes, amplitudes, offsets, counts):
    pattern_side = probe_modes.shape[-1]
    rim_width = pattern_side // 2
    slice_count = object_field.shape[1]
    tile_cells = object_field.shape[-1]
    slot_count = amplitudes.shape[1]
    ext_side = tile_cells + 2 * rim_width
    dft_table = tables(pattern_side)
    current = object_field
    probe_total = jnp.zeros(probe_modes.shape, jnp.float32)
    for batch_index in range(amplitudes.shape[0]):
        extended = with_halo(current, (("row", 2), ("col", 3)), rim_width)
        batch_amplitudes = amplitudes[batch_index, :, 0]
        batch_rows = offsets[batch_index, 0, :, 0]
        batch_cols = offsets[batch_index, 1, :, 0]
        slot_limit = counts[batch_index, 0, 0]

        def slot_terms(slot_index):
            start_row = batch_rows[slot_index]
            start_col = batch_cols[slot_index]
            zero_index = jnp.zeros((), jnp.int32)
            anchor = (zero_index, zero_index, start_row, start_col)
            patch_cells = lax.dynamic_slice(
                extended, anchor, (2, slice_count, pattern_side, pattern_side)
            )
            amplitude = lax.dynamic_index_in_dim(batch_amplitudes, slot_index, 0, keepdims=False)
            object_stack, probe_stack = position_terms(
                patch_cells, probe_modes, amplitude, dft_table
            )
            return (anchor, object_stack, probe_stack)

        def accumulate(running, anchor, object_stack, probe_stack):
            gradient, probe_part = running
            window = lax.dynamic_slice(gradient, anchor, object_stack.shape)
            gradient = lax.dynamic_update_slice(gradient, window + object_stack, anchor)
            return (gradient, probe_part + probe_stack)

        def visit_masked(slot_index, running):
            anchor, object_stack, probe_stack = slot_terms(slot_index)
            weight = (slot_index < slot_limit).astype(jnp.float32)
            return accumulate(running, anchor, object_stack * weight, probe_stack * weight)

        running = (
            jnp.zeros((2, slice_count, ext_side, ext_side), jnp.float32),
            jnp.zeros(probe_modes.shape, jnp.float32),
        )
        running = lax.fori_loop(0, slot_count, visit_masked, running)
        gradient, probe_part = running
        tile_grad = return_sectioned(gradient, rim_width, tile_cells)
        current = current - OBJECT_STEP * tile_grad
        probe_total = probe_total + lax.psum(probe_part, ("row", "col"))
    return (current, probe_modes - PROBE_STEP * probe_total)


def solution(mesh):
    return jax.shard_map(
        body,
        mesh=mesh,
        in_specs=(
            P(None, None, "row", "col"),
            P(),
            P(None, "row", "col", None, None),
            P(None, None, "row", "col"),
            P(None, "row", "col"),
        ),
        out_specs=(P(None, None, "row", "col"), P()),
        check_vma=False,
    )
```

profile of v0, /device:TPU:1, one launch (start us, length us, event | category | flops | bytes accessed | tf_op | source)
XLA Modules:
  0.0 909.7 jit_solution(2415965093989044361)
XLA Ops:
  8.9 5.7 collective-permute-start
  16.0 9.1 collective-permute-done
  25.1 13.4 %collective-permute-done.1 = f32[2,2,128,256]{2,3,1,0:T(8,128)S(1)} collective-permute-done((f32[2,2,128,256]{2,3,1,0:T(8,128)S(1)}, f32[2,2,128,256]{2,3,1,0:T(8,128)S(1)}, u32[]{:S(2)}, u32[]{:S(2)}) %collective-permute-start.1) | collective-permute-done | bytes 524320 | tf_op jit(solution)/shard_map/ppermute | solution.py:26
  40.3 4.7 collective-permute-start.2
  57.0 4.4 collective-permute-done.3
  68.1 272.4 %while.46 = (s32[]{:T(128)}, f32[2,2,512,512]{3,2,1,0:T(8,128)}, f32[2,2,256,256]{2,3,1,0:T(8,128)}, s32[3]{0:T(128)S(1)}, s32[3]{0:T(128)S(1)}, /*index=5*/f32[...) while((s32[]{:T(128)}, f32[2,2,512,512]{3,2,1,0:T(8,128)}, ...), condition=%wide.region_6.7_spmd.clone.clone.clone.clone, body=%wide.region_0.6_spmd.clone.clone.clone.clone.sunk | while | flops 3292069888 | bytes 88081760 | solution.py:187
  145.7 12.0 %dynamic_update_slice.24 = f32[2,2,512,512]{3,2,1,0:T(8,128)} dynamic-update-slice(f32[2,2,512,512]{3,2,1,0:T(8,128)} %get-tuple-element.1607, f32[2,2,256,256]{3,2,1,0:T(8,128)S(1)} %copy.239, s32[]{:T(128)} %constant.326.clone.1..sunk, s32[]{:T(128)} %constant.326.clone.1..sunk, s32[]{:T(128)S(6)} %select_n.701, s32[]{:T(128)S(6)} %select_n.702) | dynamic-update-slice | bytes 2097156 | tf_op jit(solution)/shard_map/while/body/eval_jaxpr/dynamic_update_slice | solution.py:175
  235.6 11.7 %dynamic_update_slice.24 = f32[2,2,512,512]{3,2,1,0:T(8,128)} dynamic-update-slice(f32[2,2,512,512]{3,2,1,0:T(8,128)} %get-tuple-element.1607, f32[2,2,256,256]{3,2,1,0:T(8,128)S(1)} %copy.239, s32[]{:T(128)} %constant.326.clone.1..sunk, s32[]{:T(128)} %constant.326.clone.1..sunk, s32[]{:T(128)S(6)} %select_n.701, s32[]{:T(128)S(6)} %select_n.702) | dynamic-update-slice | bytes 2097156 | tf_op jit(solution)/shard_map/while/body/eval_jaxpr/dynamic_update_slice | solution.py:175
  325.0 11.9 %dynamic_update_slice.24 = f32[2,2,512,512]{3,2,1,0:T(8,128)} dynamic-update-slice(f32[2,2,512,512]{3,2,1,0:T(8,128)} %get-tuple-element.1607, f32[2,2,256,256]{3,2,1,0:T(8,128)S(1)} %copy.239, s32[]{:T(128)} %constant.326.clone.1..sunk, s32[]{:T(128)} %constant.326.clone.1..sunk, s32[]{:T(128)S(6)} %select_n.701, s32[]{:T(128)S(6)} %select_n.702) | dynamic-update-slice | bytes 2097156 | tf_op jit(solution)/shard_map/while/body/eval_jaxpr/dynamic_update_slice | solution.py:175
  347.1 9.0 collective-permute-done.4
  360.8 5.6 collective-permute-start.6
  367.9 4.7 collective-permute-done.6
  372.6 13.3 %collective-permute-done.7 = f32[2,2,128,256]{3,2,1,0:T(8,128)S(1)} collective-permute-done((f32[2,2,128,256]{3,2,1,0:T(8,128)S(1)}, f32[2,2,128,256]{3,2,1,0:T(8,128)S(1)}, u32[]{:S(2)}, u32[]{:S(2)}) %collective-permute-start.7) | collective-permute-done | bytes 524320 | tf_op jit(solution)/shard_map/ppermute | solution.py:15
  386.3 4.7 collective-permute-start.8
  392.4 6.5 collective-permute-done.8
  398.9 14.4 %collective-permute-done.9 = f32[2,2,128,256]{3,2,1,0:T(8,128)S(1)} collective-permute-done((f32[2,2,128,256]{3,2,1,0:T(8,128)S(1)}, f32[2,2,128,256]{3,2,1,0:T(8,128)S(1)}, u32[]{:S(2)}, u32[]{:S(2)}) %collective-permute-start.9) | collective-permute-done | bytes 524320 | tf_op jit(solution)/shard_map/ppermute | solution.py:26
  415.0 9.9 %collective-permute-start.10 = (f32[2,2,512,128]{3,2,1,0:T(8,128)}, f32[2,2,512,128]{3,2,1,0:T(8,128)}, u32[]{:S(2)}, u32[]{:S(2)}) collective-permute-start(f32[2,2,512,128]{3,2,1,0:T(8,128)} %get-tuple-element.1344), channel_id=1, source_target_pairs={{0,1},{1,2},{2,3},{3,4},{4,5},{5,6},{6,7},{7,8},{8,9},{9,10},{10,1... | collective-permute-start | bytes 3145736 | tf_op jit(solution)/shard_map/ppermute | solution.py:25
  428.0 8.9 collective-permute-done.10
  448.1 273.8 %while.47 = (s32[]{:T(128)}, f32[2,2,512,512]{3,2,1,0:T(8,128)}, f32[2,2,256,256]{2,3,1,0:T(8,128)}, s32[3]{0:T(128)S(1)}, s32[3]{0:T(128)S(1)}, /*index=5*/f32[...) while((s32[]{:T(128)}, f32[2,2,512,512]{3,2,1,0:T(8,128)}, ...), condition=%wide.region_13.14_spmd.clone.clone.clone.clone, body=%wide.region_7.13_spmd.clone.clone.clone.clone.sunk | while | flops 3292069888 | bytes 83887400 | solution.py:187
  526.6 11.6 %dynamic_update_slice.25 = f32[2,2,512,512]{3,2,1,0:T(8,128)} dynamic-update-slice(f32[2,2,512,512]{3,2,1,0:T(8,128)} %get-tuple-element.1649, f32[2,2,256,256]{3,2,1,0:T(8,128)S(1)} %copy.245, s32[]{:T(128)} %constant.326.clone.1..sunk.1, s32[]{:T(128)} %constant.326.clone.1..sunk.1, s32[]{:T(128)S(6)} %select_n.752, s32[]{:T(128)S(6)} %select_n.753) | dynamic-update-slice | bytes 2097156 | tf_op jit(solution)/shard_map/while/body/eval_jaxpr/dynamic_update_slice | solution.py:175
  616.9 11.9 %dynamic_update_slice.25 = f32[2,2,512,512]{3,2,1,0:T(8,128)} dynamic-update-slice(f32[2,2,512,512]{3,2,1,0:T(8,128)} %get-tuple-element.1649, f32[2,2,256,256]{3,2,1,0:T(8,128)S(1)} %copy.245, s32[]{:T(128)} %constant.326.clone.1..sunk.1, s32[]{:T(128)} %constant.326.clone.1..sunk.1, s32[]{:T(128)S(6)} %select_n.752, s32[]{:T(128)S(6)} %select_n.753) | dynamic-update-slice | bytes 2097156 | tf_op jit(solution)/shard_map/while/body/eval_jaxpr/dynamic_update_slice | solution.py:175
  707.6 11.6 %dynamic_update_slice.25 = f32[2,2,512,512]{3,2,1,0:T(8,128)} dynamic-update-slice(f32[2,2,512,512]{3,2,1,0:T(8,128)} %get-tuple-element.1649, f32[2,2,256,256]{3,2,1,0:T(8,128)S(1)} %copy.245, s32[]{:T(128)} %constant.326.clone.1..sunk.1, s32[]{:T(128)} %constant.326.clone.1..sunk.1, s32[]{:T(128)S(6)} %select_n.752, s32[]{:T(128)S(6)} %select_n.753) | dynamic-update-slice | bytes 2097156 | tf_op jit(solution)/shard_map/while/body/eval_jaxpr/dynamic_update_slice | solution.py:175
  746.1 6.2 collective-permute-start.14
  753.7 142.7 %all-reduce.2.cloned.1.call-done = f32[2,2,256,256]{3,2,1,0:T(8,128)} async-done(((f32[2,2,256,256]{3,2,1,0:T(8,128)}), f32[2,2,256,256]{3,2,1,0:T(8,128)}) %all-reduce.2.cloned.1.call-update) | async-done | bytes 1048592 | tf_op jit(solution)/shard_map/psum | solution.py:191
  (481 shorter events, 526.5 us)
Async XLA Ops:
  7.2 889.3 %all-reduce.2.cloned.1.call-start = ((), (), s32[]{:S(2)}) async-start(), calls=%async_computation | async-start | bytes 2097152 | tf_op jit(solution)/shard_map/psum | solution.py:191
  8.9 16.2 %collective-permute-start = (f32[2,2,128,256]{2,3,1,0:T(8,128)S(1)}, f32[2,2,128,256]{2,3,1,0:T(8,128)S(1)}, u32[]{:S(2)}, u32[]{:S(2)}) collective-permute-start(f32[2,2,128,256]{2,3,1,0:T(8,128)S(1)} %get-tuple-element.1354), channel_id=1, source_target_pairs={{0,16},{16,32},{32,48},{48,64},{64,80},{80,96},{96,112},{1,17},{17... | collective-permute-start | bytes 1572872 | tf_op jit(solution)/shard_map/ppermute | solution.py:25
  14.5 32.4 %copy-start.9 = (f32[2,2,256,256]{3,2,1,0:T(8,128)S(1)}, f32[2,2,256,256]{3,2,1,0:T(8,128)}, u32[]{:S(2)}) copy-start(f32[2,2,256,256]{3,2,1,0:T(8,128)} %param.26) | copy-start | bytes 3145732
  14.6 23.9 %collective-permute-start.1 = (f32[2,2,128,256]{2,3,1,0:T(8,128)S(1)}, f32[2,2,128,256]{2,3,1,0:T(8,128)S(1)}, u32[]{:S(2)}, u32[]{:S(2)}) collective-permute-start(f32[2,2,128,256]{2,3,1,0:T(8,128)S(1)} %get-tuple-element.1355), channel_id=1, source_target_pairs={{16,0},{32,16},{48,32},{64,48},{80,64},{96,80},{112,96},{17,1},{33... | collective-permute-start | bytes 1572872 | tf_op jit(solution)/shard_map/ppermute | solution.py:26
  40.3 16.7 %collective-permute-start.2 = (f32[2,2,512,128]{2,3,1,0:T(8,128)}, f32[2,2,512,128]{2,3,1,0:T(8,128)}, u32[]{:S(2)}, u32[]{:S(2)}) collective-permute-start(f32[2,2,512,128]{2,3,1,0:T(8,128)} %get-tuple-element.1348), channel_id=1, source_target_pairs={{0,1},{1,2},{2,3},{3,4},{4,5},{5,6},{6,7},{7,8},{8,9},{9,10},{10,1... | collective-permute-start | bytes 3145736 | tf_op jit(solution)/shard_map/ppermute | solution.py:25
  45.0 16.4 %collective-permute-start.3 = (f32[2,2,512,128]{2,3,1,0:T(8,128)}, f32[2,2,512,128]{2,3,1,0:T(8,128)}, u32[]{:S(2)}, u32[]{:S(2)}) collective-permute-start(f32[2,2,512,128]{2,3,1,0:T(8,128)} %get-tuple-element.1349), channel_id=1, source_target_pairs={{1,0},{2,1},{3,2},{4,3},{5,4},{6,5},{7,6},{8,7},{9,8},{10,9},{11,1... | collective-permute-start | bytes 3145736 | tf_op jit(solution)/shard_map/ppermute | solution.py:26
  68.6 37.8 %copy-start.6 = (f32[3,256,256]{1,2,0:T(8,128)}, f32[3,256,256]{1,2,0:T(8,128)S(1)}, u32[]{:S(2)}) copy-start(f32[3,256,256]{1,2,0:T(8,128)S(1)} %get-tuple-element.1627) | copy-start | bytes 2359300 | tf_op jit(solution)/shard_map/while
  157.9 38.0 %copy-start.6 = (f32[3,256,256]{1,2,0:T(8,128)}, f32[3,256,256]{1,2,0:T(8,128)S(1)}, u32[]{:S(2)}) copy-start(f32[3,256,256]{1,2,0:T(8,128)S(1)} %get-tuple-element.1627) | copy-start | bytes 2359300 | tf_op jit(solution)/shard_map/while
  247.5 38.0 %copy-start.6 = (f32[3,256,256]{1,2,0:T(8,128)}, f32[3,256,256]{1,2,0:T(8,128)S(1)}, u32[]{:S(2)}) copy-start(f32[3,256,256]{1,2,0:T(8,128)S(1)} %get-tuple-element.1627) | copy-start | bytes 2359300 | tf_op jit(solution)/shard_map/while
  342.3 13.8 %collective-permute-start.4 = (f32[2,2,512,128]{3,2,1,0:T(8,128)S(1)}, f32[2,2,512,128]{3,2,1,0:T(8,128)S(1)}, u32[]{:S(2)}, u32[]{:S(2)}) collective-permute-start(f32[2,2,512,128]{3,2,1,0:T(8,128)S(1)} %get-tuple-element.1341), channel_id=1, source_target_pairs={{0,1},{1,2},{2,3},{3,4},{4,5},{5,6},{6,7},{7,8},{8,9},{9,10},{10,1... | collective-permute-start | bytes 3145736 | tf_op jit(solution)/shard_map/ppermute | solution.py:15
  344.4 16.1 %collective-permute-start.5 = (f32[2,2,512,128]{3,2,1,0:T(8,128)S(1)}, f32[2,2,512,128]{3,2,1,0:T(8,128)S(1)}, u32[]{:S(2)}, u32[]{:S(2)}) collective-permute-start(f32[2,2,512,128]{3,2,1,0:T(8,128)S(1)} %get-tuple-element.1340), channel_id=1, source_target_pairs={{1,0},{2,1},{3,2},{4,3},{5,4},{6,5},{7,6},{8,7},{9,8},{10,9},{11,1... | collective-permute-start | bytes 3145736 | tf_op jit(solution)/shard_map/ppermute | solution.py:15
  360.8 11.7 %collective-permute-start.6 = (f32[2,2,128,256]{3,2,1,0:T(8,128)S(1)}, f32[2,2,128,256]{3,2,1,0:T(8,128)S(1)}, u32[]{:S(2)}, u32[]{:S(2)}) collective-permute-start(f32[2,2,128,256]{3,2,1,0:T(8,128)S(1)} %get-tuple-element.1347), channel_id=1, source_target_pairs={{0,16},{16,32},{32,48},{48,64},{64,80},{80,96},{96,112},{1,17},{17... | collective-permute-start | bytes 1572872 | tf_op jit(solution)/shard_map/ppermute | solution.py:15
  366.5 19.4 %collective-permute-start.7 = (f32[2,2,128,256]{3,2,1,0:T(8,128)S(1)}, f32[2,2,128,256]{3,2,1,0:T(8,128)S(1)}, u32[]{:S(2)}, u32[]{:S(2)}) collective-permute-start(f32[2,2,128,256]{3,2,1,0:T(8,128)S(1)} %get-tuple-element.1346), channel_id=1, source_target_pairs={{16,0},{32,16},{48,32},{64,48},{80,64},{96,80},{112,96},{17,1},{33... | collective-permute-start | bytes 1572872 | tf_op jit(solution)/shard_map/ppermute | solution.py:15
  386.2 55.2 %copy-start.3 = (f32[2,2,256,256]{3,2,1,0:T(8,128)}, f32[2,2,256,256]{3,2,1,0:T(8,128)S(1)}, u32[]{:S(2)}) copy-start(f32[2,2,256,256]{3,2,1,0:T(8,128)S(1)} %multiply_subtract_fusion.2) | copy-start | bytes 3145732
  386.3 12.7 %collective-permute-start.8 = (f32[2,2,128,256]{3,2,1,0:T(8,128)S(1)}, f32[2,2,128,256]{3,2,1,0:T(8,128)S(1)}, u32[]{:S(2)}, u32[]{:S(2)}) collective-permute-start(f32[2,2,128,256]{3,2,1,0:T(8,128)S(1)} %get-tuple-element.1352), channel_id=1, source_target_pairs={{0,16},{16,32},{32,48},{48,64},{64,80},{80,96},{96,112},{1,17},{17... | collective-permute-start | bytes 1572872 | tf_op jit(solution)/shard_map/ppermute | solution.py:25
  391.0 35.9 %copy-start.11 = (f32[1,3,1,256,256]{4,3,2,1,0:T(8,128)S(1)}, f32[1,3,1,256,256]{4,3,2,1,0:T(8,128)}, u32[]{:S(2)}) copy-start(f32[1,3,1,256,256]{4,3,2,1,0:T(8,128)} %get-tuple-element.1350) | copy-start | bytes 2359300
  391.0 22.3 %collective-permute-start.9 = (f32[2,2,128,256]{3,2,1,0:T(8,128)S(1)}, f32[2,2,128,256]{3,2,1,0:T(8,128)S(1)}, u32[]{:S(2)}, u32[]{:S(2)}) collective-permute-start(f32[2,2,128,256]{3,2,1,0:T(8,128)S(1)} %get-tuple-element.1353), channel_id=1, source_target_pairs={{16,0},{32,16},{48,32},{64,48},{80,64},{96,80},{112,96},{17,1},{33... | collective-permute-start | bytes 1572872 | tf_op jit(solution)/shard_map/ppermute | solution.py:26
  415.0 21.9 %collective-permute-start.10 = (f32[2,2,512,128]{3,2,1,0:T(8,128)}, f32[2,2,512,128]{3,2,1,0:T(8,128)}, u32[]{:S(2)}, u32[]{:S(2)}) collective-permute-start(f32[2,2,512,128]{3,2,1,0:T(8,128)} %get-tuple-element.1344), channel_id=1, source_target_pairs={{0,1},{1,2},{2,3},{3,4},{4,5},{5,6},{6,7},{7,8},{8,9},{9,10},{10,1... | collective-permute-start | bytes 3145736 | tf_op jit(solution)/shard_map/ppermute | solution.py:25
  424.9 16.4 %collective-permute-start.11 = (f32[2,2,512,128]{3,2,1,0:T(8,128)}, f32[2,2,512,128]{3,2,1,0:T(8,128)}, u32[]{:S(2)}, u32[]{:S(2)}) collective-permute-start(f32[2,2,512,128]{3,2,1,0:T(8,128)} %get-tuple-element.1345), channel_id=1, source_target_pairs={{1,0},{2,1},{3,2},{4,3},{5,4},{6,5},{7,6},{8,7},{9,8},{10,9},{11,1... | collective-permute-start | bytes 3145736 | tf_op jit(solution)/shard_map/ppermute | solution.py:26
  725.0 14.2 %collective-permute-start.12 = (f32[2,2,512,128]{3,2,1,0:T(8,128)}, f32[2,2,512,128]{3,2,1,0:T(8,128)}, u32[]{:S(2)}, u32[]{:S(2)}) collective-permute-start(f32[2,2,512,128]{3,2,1,0:T(8,128)} %get-tuple-element.1339), channel_id=1, source_target_pairs={{0,1},{1,2},{2,3},{3,4},{4,5},{5,6},{6,7},{7,8},{8,9},{9,10},{10,1... | collective-permute-start | bytes 3145736 | tf_op jit(solution)/shard_map/ppermute | solution.py:15
  727.2 16.4 %collective-permute-start.13 = (f32[2,2,512,128]{3,2,1,0:T(8,128)}, f32[2,2,512,128]{3,2,1,0:T(8,128)}, u32[]{:S(2)}, u32[]{:S(2)}) collective-permute-start(f32[2,2,512,128]{3,2,1,0:T(8,128)} %get-tuple-element.1338), channel_id=1, source_target_pairs={{1,0},{2,1},{3,2},{4,3},{5,4},{6,5},{7,6},{8,7},{9,8},{10,9},{11,1... | collective-permute-start | bytes 3145736 | tf_op jit(solution)/shard_map/ppermute | solution.py:15
  746.1 153.1 %collective-permute-start.14 = (f32[2,2,128,256]{3,2,1,0:T(8,128)}, f32[2,2,128,256]{3,2,1,0:T(8,128)}, u32[]{:S(2)}, u32[]{:S(2)}) collective-permute-start(f32[2,2,128,256]{3,2,1,0:T(8,128)} %get-tuple-element.1343), channel_id=1, source_target_pairs={{0,16},{16,32},{32,48},{48,64},{64,80},{80,96},{96,112},{1,17},{17... | collective-permute-start | bytes 1572872 | tf_op jit(solution)/shard_map/ppermute | solution.py:15
  752.3 149.2 %copy-start.4 = (f32[2,2,256,256]{3,2,1,0:T(8,128)S(1)}, f32[2,2,256,256]{3,2,1,0:T(8,128)}, u32[]{:S(2)}) copy-start(f32[2,2,256,256]{3,2,1,0:T(8,128)} %copy-done.3) | copy-start | bytes 3145732
  752.3 148.0 %collective-permute-start.15 = (f32[2,2,128,256]{3,2,1,0:T(8,128)}, f32[2,2,128,256]{3,2,1,0:T(8,128)}, u32[]{:S(2)}, u32[]{:S(2)}) collective-permute-start(f32[2,2,128,256]{3,2,1,0:T(8,128)} %get-tuple-element.1342), channel_id=1, source_target_pairs={{16,0},{32,16},{48,32},{64,48},{80,64},{96,80},{112,96},{17,1},{33... | collective-permute-start | bytes 1572872 | tf_op jit(solution)/shard_map/ppermute | solution.py:15
  (17 other events, 159.1 us)
Sparse Core Ops, SparseCore 0:
  738.9 157.5 all-reduce.1
where the time goes:
time: 916 us; the launch traced here: 910 us
  matrix products  358 us (39%)
  waiting for transfers between devices  243 us (27%)
  local copies, waits for them, and re-layouts  141 us (15%)
  other arithmetic  62.3 us (7%)
  starting transfers between devices  56.1 us (6%)
  loops' own time  34.6 us (4%)
  between operations  14.7 us (2%)
    dot_general x288, matrix products, contract(): return jnp.einsum(form, left, right, preferred_element_type=jnp.float32)  358 us
    psum x1, waiting for transfers between devices, body(): probe_total = probe_total + lax.psum(probe_part, ('row', 'col'))  143 us
    dynamic_update_slice x12, local copies, waits for them, and re-layouts, accumulate(): gradient = lax.dynamic_update_slice(gradient, window + object_stack, anchor)  80.3 us
    ppermute x4, waiting for transfers between devices, with_halo(): after = lax.ppermute(leading, axis, down)  36.6 us
    another operation x2, loops' own time, body(): running = lax.fori_loop(0, slot_count, visit_masked, running)  34.6 us
    ppermute x8, waiting for transfers between devices, from_behind(): lax.ppermute(value, axis, [(source, source + steps) for source in range(l...  34.3 us
    ppermute x4, waiting for transfers between devices, with_halo(): before = lax.ppermute(last, axis, up)  28.9 us
    ppermute x4, starting transfers between devices, with_halo(): before = lax.ppermute(last, axis, up)  24.9 us
  transfers between devices with their start and end apart: 17, of which 15 were waited for; matrix products, arithmetic and copies ran while one was open for 3% of the time, Pallas kernels for 0%

commit v1 on v0

--- a/solution.py
+++ b/solution.py
@@ -1,12 +1,23 @@
+import functools
 import math
 import jax
 import jax.numpy as jnp
 from jax import lax
 from jax.sharding import PartitionSpec as P
+from jax.lax import psum
 
 AMPLITUDE_FLOOR = 0.5
 OBJECT_STEP = 0.25
 PROBE_STEP = 0.125
+
+
+def supply_the_sheets(field_in, a_name, shard_axis):
+    for to_i in (a_name, shard_axis):
+        field_in = psum(field_in, axis_name=to_i)
+    return field_in
+
+
+take_pipes = functools.partial(supply_the_sheets, a_name="row", shard_axis="col")
 
 
 def from_behind(value, axis, steps):
@@ -188,7 +199,7 @@
         gradient, probe_part = running
         tile_grad = return_sectioned(gradient, rim_width, tile_cells)
         current = current - OBJECT_STEP * tile_grad
-        probe_total = probe_total + lax.psum(probe_part, ("row", "col"))
+        probe_total = probe_total + take_pipes(probe_part)
     return (current, probe_modes - PROBE_STEP * probe_total)
 
 

time: 916 us -> 972 us (1.061)
  waiting for transfers between devices: 243 us -> 297 us
    psum x1 -> x2, waiting for transfers between devices: 143 us -> 197 us  [supply_the_sheets(): field_in = psum(field_in, axis_name=to_i)]
  transfers between devices with their start and end apart: 17 -> 18, of which waited for: 15 -> 16; matrix products, arithmetic and copies ran while one was open for 3% -> 2% of each run, Pallas kernels for 0% -> 0%
where the time goes in v1:
time: 972 us; the launch traced here: 966 us
  matrix products  358 us (37%)
  waiting for transfers between devices  297 us (31%)
  local copies, waits for them, and re-layouts  141 us (15%)
  other arithmetic  62.1 us (6%)
  starting transfers between devices  55.9 us (6%)
  loops' own time  36.3 us (4%)
  between operations  14.8 us (2%)
    dot_general x288, matrix products, contract(): return jnp.einsum(form, left, right, preferred_element_type=jnp.float32)  358 us
    psum x2, waiting for transfers between devices, supply_the_sheets(): field_in = psum(field_in, axis_name=to_i)  197 us
    dynamic_update_slice x12, local copies, waits for them, and re-layouts, accumulate(): gradient = lax.dynamic_update_slice(gradient, window + object_stack, anchor)  80.3 us
    ppermute x4, waiting for transfers between devices, with_halo(): after = lax.ppermute(leading, axis, down)  36.7 us
    another operation x2, loops' own time, body(): running = lax.fori_loop(0, slot_count, visit_masked, running)  36.3 us
    ppermute x8, waiting for transfers between devices, from_behind(): lax.ppermute(value, axis, [(source, source + steps) for source in range(l...  34.3 us
    ppermute x4, waiting for transfers between devices, with_halo(): before = lax.ppermute(last, axis, up)  28.8 us
    ppermute x4, starting transfers between devices, with_halo(): before = lax.ppermute(last, axis, up)  24.9 us
  transfers between devices with their start and end apart: 18, of which 16 were waited for; matrix products, arithmetic and copies ran while one was open for 2% of the time, Pallas kernels for 0%

profile of v1, /device:TPU:1, one launch (start us, length us, event | category | flops | bytes accessed | tf_op | source)
XLA Modules:
  0.0 965.8 jit_solution(12078481909129152768)
XLA Ops:
  8.9 5.7 collective-permute-start
  16.0 9.1 collective-permute-done
  25.1 13.4 %collective-permute-done.1 = f32[2,2,128,256]{2,3,1,0:T(8,128)S(1)} collective-permute-done((f32[2,2,128,256]{2,3,1,0:T(8,128)S(1)}, f32[2,2,128,256]{2,3,1,0:T(8,128)S(1)}, u32[]{:S(2)}, u32[]{:S(2)}) %collective-permute-start.1) | collective-permute-done | bytes 524320 | tf_op jit(solution)/shard_map/ppermute | solution.py:37
  40.3 4.7 collective-permute-start.2
  68.1 272.6 %while.46 = (s32[]{:T(128)}, f32[2,2,512,512]{3,2,1,0:T(8,128)}, f32[2,2,256,256]{2,3,1,0:T(8,128)}, s32[3]{0:T(128)S(1)}, s32[3]{0:T(128)S(1)}, /*index=5*/f32[...) while((s32[]{:T(128)}, f32[2,2,512,512]{3,2,1,0:T(8,128)}, ...), condition=%wide.region_6.7_spmd.clone.clone.clone.clone, body=%wide.region_0.6_spmd.clone.clone.clone.clone.sunk | while | flops 3292069888 | bytes 88081760 | solution.py:198
  145.8 12.0 %dynamic_update_slice.24 = f32[2,2,512,512]{3,2,1,0:T(8,128)} dynamic-update-slice(f32[2,2,512,512]{3,2,1,0:T(8,128)} %get-tuple-element.1607, f32[2,2,256,256]{3,2,1,0:T(8,128)S(1)} %copy.239, s32[]{:T(128)} %constant.326.clone.1..sunk, s32[]{:T(128)} %constant.326.clone.1..sunk, s32[]{:T(128)S(6)} %select_n.701, s32[]{:T(128)S(6)} %select_n.702) | dynamic-update-slice | bytes 2097156 | tf_op jit(solution)/shard_map/while/body/eval_jaxpr/dynamic_update_slice | solution.py:186
  235.8 11.7 %dynamic_update_slice.24 = f32[2,2,512,512]{3,2,1,0:T(8,128)} dynamic-update-slice(f32[2,2,512,512]{3,2,1,0:T(8,128)} %get-tuple-element.1607, f32[2,2,256,256]{3,2,1,0:T(8,128)S(1)} %copy.239, s32[]{:T(128)} %constant.326.clone.1..sunk, s32[]{:T(128)} %constant.326.clone.1..sunk, s32[]{:T(128)S(6)} %select_n.701, s32[]{:T(128)S(6)} %select_n.702) | dynamic-update-slice | bytes 2097156 | tf_op jit(solution)/shard_map/while/body/eval_jaxpr/dynamic_update_slice | solution.py:186
  325.2 11.9 %dynamic_update_slice.24 = f32[2,2,512,512]{3,2,1,0:T(8,128)} dynamic-update-slice(f32[2,2,512,512]{3,2,1,0:T(8,128)} %get-tuple-element.1607, f32[2,2,256,256]{3,2,1,0:T(8,128)S(1)} %copy.239, s32[]{:T(128)} %constant.326.clone.1..sunk, s32[]{:T(128)} %constant.326.clone.1..sunk, s32[]{:T(128)S(6)} %select_n.701, s32[]{:T(128)S(6)} %select_n.702) | dynamic-update-slice | bytes 2097156 | tf_op jit(solution)/shard_map/while/body/eval_jaxpr/dynamic_update_slice | solution.py:186
  347.3 9.0 collective-permute-done.4
  361.0 5.6 collective-permute-start.6
  368.0 4.7 collective-permute-done.6
  372.8 13.3 %collective-permute-done.7 = f32[2,2,128,256]{3,2,1,0:T(8,128)S(1)} collective-permute-done((f32[2,2,128,256]{3,2,1,0:T(8,128)S(1)}, f32[2,2,128,256]{3,2,1,0:T(8,128)S(1)}, u32[]{:S(2)}, u32[]{:S(2)}) %collective-permute-start.7) | collective-permute-done | bytes 524320 | tf_op jit(solution)/shard_map/ppermute | solution.py:26
  386.5 4.7 collective-permute-start.8
  392.6 6.4 collective-permute-done.8
  399.0 14.5 %collective-permute-done.9 = f32[2,2,128,256]{3,2,1,0:T(8,128)S(1)} collective-permute-done((f32[2,2,128,256]{3,2,1,0:T(8,128)S(1)}, f32[2,2,128,256]{3,2,1,0:T(8,128)S(1)}, u32[]{:S(2)}, u32[]{:S(2)}) %collective-permute-start.9) | collective-permute-done | bytes 524320 | tf_op jit(solution)/shard_map/ppermute | solution.py:37
  415.3 9.8 %collective-permute-start.10 = (f32[2,2,512,128]{3,2,1,0:T(8,128)}, f32[2,2,512,128]{3,2,1,0:T(8,128)}, u32[]{:S(2)}, u32[]{:S(2)}) collective-permute-start(f32[2,2,512,128]{3,2,1,0:T(8,128)} %get-tuple-element.1344), channel_id=1, source_target_pairs={{0,1},{1,2},{2,3},{3,4},{4,5},{5,6},{6,7},{7,8},{8,9},{9,10},{10,1... | collective-permute-start | bytes 3145736 | tf_op jit(solution)/shard_map/ppermute | solution.py:36
  428.2 8.9 collective-permute-done.10
  448.2 275.5 %while.47 = (s32[]{:T(128)}, f32[2,2,512,512]{3,2,1,0:T(8,128)}, f32[2,2,256,256]{2,3,1,0:T(8,128)}, s32[3]{0:T(128)S(1)}, s32[3]{0:T(128)S(1)}, /*index=5*/f32[...) while((s32[]{:T(128)}, f32[2,2,512,512]{3,2,1,0:T(8,128)}, ...), condition=%wide.region_13.14_spmd.clone.clone.clone.clone, body=%wide.region_7.13_spmd.clone.clone.clone.clone.sunk | while | flops 3292069888 | bytes 83887400 | solution.py:198
  527.3 11.6 %dynamic_update_slice.25 = f32[2,2,512,512]{3,2,1,0:T(8,128)} dynamic-update-slice(f32[2,2,512,512]{3,2,1,0:T(8,128)} %get-tuple-element.1649, f32[2,2,256,256]{3,2,1,0:T(8,128)S(1)} %copy.245, s32[]{:T(128)} %constant.326.clone.1..sunk.1, s32[]{:T(128)} %constant.326.clone.1..sunk.1, s32[]{:T(128)S(6)} %select_n.752, s32[]{:T(128)S(6)} %select_n.753) | dynamic-update-slice | bytes 2097156 | tf_op jit(solution)/shard_map/while/body/eval_jaxpr/dynamic_update_slice | solution.py:186
  618.2 11.9 %dynamic_update_slice.25 = f32[2,2,512,512]{3,2,1,0:T(8,128)} dynamic-update-slice(f32[2,2,512,512]{3,2,1,0:T(8,128)} %get-tuple-element.1649, f32[2,2,256,256]{3,2,1,0:T(8,128)S(1)} %copy.245, s32[]{:T(128)} %constant.326.clone.1..sunk.1, s32[]{:T(128)} %constant.326.clone.1..sunk.1, s32[]{:T(128)S(6)} %select_n.752, s32[]{:T(128)S(6)} %select_n.753) | dynamic-update-slice | bytes 2097156 | tf_op jit(solution)/shard_map/while/body/eval_jaxpr/dynamic_update_slice | solution.py:186
  709.5 11.6 %dynamic_update_slice.25 = f32[2,2,512,512]{3,2,1,0:T(8,128)} dynamic-update-slice(f32[2,2,512,512]{3,2,1,0:T(8,128)} %get-tuple-element.1649, f32[2,2,256,256]{3,2,1,0:T(8,128)S(1)} %copy.245, s32[]{:T(128)} %constant.326.clone.1..sunk.1, s32[]{:T(128)} %constant.326.clone.1..sunk.1, s32[]{:T(128)S(6)} %select_n.752, s32[]{:T(128)S(6)} %select_n.753) | dynamic-update-slice | bytes 2097156 | tf_op jit(solution)/shard_map/while/body/eval_jaxpr/dynamic_update_slice | solution.py:186
  748.0 6.2 collective-permute-start.14
  755.5 76.6 %all-reduce.5.cloned.1.call-done = f32[2,2,256,256]{3,2,1,0:T(8,128)} async-done(((f32[2,2,256,256]{3,2,1,0:T(8,128)}), f32[2,2,256,256]{3,2,1,0:T(8,128)}) %all-reduce.5.cloned.1.call-update) | async-done | bytes 1048592 | tf_op jit(solution)/shard_map/psum | solution.py:16
  835.7 120.7 %all-reduce.3.cloned.1.call-done = f32[2,2,256,256]{3,2,1,0:T(8,128)} async-done(((f32[2,2,256,256]{3,2,1,0:T(8,128)}), f32[2,2,256,256]{3,2,1,0:T(8,128)}) %all-reduce.3.cloned.1.call-update) | async-done | bytes 1048592 | tf_op jit(solution)/shard_map/psum | solution.py:16
  (486 shorter events, 530.7 us)
Async XLA Ops:
  7.2 824.9 %all-reduce.5.cloned.1.call-start = ((), (), s32[]{:S(2)}) async-start(), calls=%async_computation.1 | async-start | bytes 2097152 | tf_op jit(solution)/shard_map/psum | solution.py:16
  8.9 16.2 %collective-permute-start = (f32[2,2,128,256]{2,3,1,0:T(8,128)S(1)}, f32[2,2,128,256]{2,3,1,0:T(8,128)S(1)}, u32[]{:S(2)}, u32[]{:S(2)}) collective-permute-start(f32[2,2,128,256]{2,3,1,0:T(8,128)S(1)} %get-tuple-element.1354), channel_id=1, source_target_pairs={{0,16},{16,32},{32,48},{48,64},{64,80},{80,96},{96,112},{1,17},{17... | collective-permute-start | bytes 1572872 | tf_op jit(solution)/shard_map/ppermute | solution.py:36
  14.6 23.9 %collective-permute-start.1 = (f32[2,2,128,256]{2,3,1,0:T(8,128)S(1)}, f32[2,2,128,256]{2,3,1,0:T(8,128)S(1)}, u32[]{:S(2)}, u32[]{:S(2)}) collective-permute-start(f32[2,2,128,256]{2,3,1,0:T(8,128)S(1)} %get-tuple-element.1355), channel_id=1, source_target_pairs={{16,0},{32,16},{48,32},{64,48},{80,64},{96,80},{112,96},{17,1},{33... | collective-permute-start | bytes 1572872 | tf_op jit(solution)/shard_map/ppermute | solution.py:37
  40.3 16.7 %collective-permute-start.2 = (f32[2,2,512,128]{2,3,1,0:T(8,128)}, f32[2,2,512,128]{2,3,1,0:T(8,128)}, u32[]{:S(2)}, u32[]{:S(2)}) collective-permute-start(f32[2,2,512,128]{2,3,1,0:T(8,128)} %get-tuple-element.1348), channel_id=1, source_target_pairs={{0,1},{1,2},{2,3},{3,4},{4,5},{5,6},{6,7},{7,8},{8,9},{9,10},{10,1... | collective-permute-start | bytes 3145736 | tf_op jit(solution)/shard_map/ppermute | solution.py:36
  45.0 16.4 %collective-permute-start.3 = (f32[2,2,512,128]{2,3,1,0:T(8,128)}, f32[2,2,512,128]{2,3,1,0:T(8,128)}, u32[]{:S(2)}, u32[]{:S(2)}) collective-permute-start(f32[2,2,512,128]{2,3,1,0:T(8,128)} %get-tuple-element.1349), channel_id=1, source_target_pairs={{1,0},{2,1},{3,2},{4,3},{5,4},{6,5},{7,6},{8,7},{9,8},{10,9},{11,1... | collective-permute-start | bytes 3145736 | tf_op jit(solution)/shard_map/ppermute | solution.py:37
  68.6 37.8 %copy-start.6 = (f32[3,256,256]{1,2,0:T(8,128)}, f32[3,256,256]{1,2,0:T(8,128)S(1)}, u32[]{:S(2)}) copy-start(f32[3,256,256]{1,2,0:T(8,128)S(1)} %get-tuple-element.1627) | copy-start | bytes 2359300 | tf_op jit(solution)/shard_map/while
  158.0 38.0 %copy-start.6 = (f32[3,256,256]{1,2,0:T(8,128)}, f32[3,256,256]{1,2,0:T(8,128)S(1)}, u32[]{:S(2)}) copy-start(f32[3,256,256]{1,2,0:T(8,128)S(1)} %get-tuple-element.1627) | copy-start | bytes 2359300 | tf_op jit(solution)/shard_map/while
  247.6 38.1 %copy-start.6 = (f32[3,256,256]{1,2,0:T(8,128)}, f32[3,256,256]{1,2,0:T(8,128)S(1)}, u32[]{:S(2)}) copy-start(f32[3,256,256]{1,2,0:T(8,128)S(1)} %get-tuple-element.1627) | copy-start | bytes 2359300 | tf_op jit(solution)/shard_map/while
  342.5 13.8 %collective-permute-start.4 = (f32[2,2,512,128]{3,2,1,0:T(8,128)S(1)}, f32[2,2,512,128]{3,2,1,0:T(8,128)S(1)}, u32[]{:S(2)}, u32[]{:S(2)}) collective-permute-start(f32[2,2,512,128]{3,2,1,0:T(8,128)S(1)} %get-tuple-element.1341), channel_id=1, source_target_pairs={{0,1},{1,2},{2,3},{3,4},{4,5},{5,6},{6,7},{7,8},{8,9},{9,10},{10,1... | collective-permute-start | bytes 3145736 | tf_op jit(solution)/shard_map/ppermute | solution.py:26
  344.6 16.1 %collective-permute-start.5 = (f32[2,2,512,128]{3,2,1,0:T(8,128)S(1)}, f32[2,2,512,128]{3,2,1,0:T(8,128)S(1)}, u32[]{:S(2)}, u32[]{:S(2)}) collective-permute-start(f32[2,2,512,128]{3,2,1,0:T(8,128)S(1)} %get-tuple-element.1340), channel_id=1, source_target_pairs={{1,0},{2,1},{3,2},{4,3},{5,4},{6,5},{7,6},{8,7},{9,8},{10,9},{11,1... | collective-permute-start | bytes 3145736 | tf_op jit(solution)/shard_map/ppermute | solution.py:26
  361.0 11.7 %collective-permute-start.6 = (f32[2,2,128,256]{3,2,1,0:T(8,128)S(1)}, f32[2,2,128,256]{3,2,1,0:T(8,128)S(1)}, u32[]{:S(2)}, u32[]{:S(2)}) collective-permute-start(f32[2,2,128,256]{3,2,1,0:T(8,128)S(1)} %get-tuple-element.1347), channel_id=1, source_target_pairs={{0,16},{16,32},{32,48},{48,64},{64,80},{80,96},{96,112},{1,17},{17... | collective-permute-start | bytes 1572872 | tf_op jit(solution)/shard_map/ppermute | solution.py:26
  366.6 19.4 %collective-permute-start.7 = (f32[2,2,128,256]{3,2,1,0:T(8,128)S(1)}, f32[2,2,128,256]{3,2,1,0:T(8,128)S(1)}, u32[]{:S(2)}, u32[]{:S(2)}) collective-permute-start(f32[2,2,128,256]{3,2,1,0:T(8,128)S(1)} %get-tuple-element.1346), channel_id=1, source_target_pairs={{16,0},{32,16},{48,32},{64,48},{80,64},{96,80},{112,96},{17,1},{33... | collective-permute-start | bytes 1572872 | tf_op jit(solution)/shard_map/ppermute | solution.py:26
  386.4 55.2 %copy-start.3 = (f32[2,2,256,256]{3,2,1,0:T(8,128)}, f32[2,2,256,256]{3,2,1,0:T(8,128)S(1)}, u32[]{:S(2)}) copy-start(f32[2,2,256,256]{3,2,1,0:T(8,128)S(1)} %multiply_subtract_fusion.2) | copy-start | bytes 3145732
  386.5 12.5 %collective-permute-start.8 = (f32[2,2,128,256]{3,2,1,0:T(8,128)S(1)}, f32[2,2,128,256]{3,2,1,0:T(8,128)S(1)}, u32[]{:S(2)}, u32[]{:S(2)}) collective-permute-start(f32[2,2,128,256]{3,2,1,0:T(8,128)S(1)} %get-tuple-element.1352), channel_id=1, source_target_pairs={{0,16},{16,32},{32,48},{48,64},{64,80},{80,96},{96,112},{1,17},{17... | collective-permute-start | bytes 1572872 | tf_op jit(solution)/shard_map/ppermute | solution.py:36
  391.2 22.4 %collective-permute-start.9 = (f32[2,2,128,256]{3,2,1,0:T(8,128)S(1)}, f32[2,2,128,256]{3,2,1,0:T(8,128)S(1)}, u32[]{:S(2)}, u32[]{:S(2)}) collective-permute-start(f32[2,2,128,256]{3,2,1,0:T(8,128)S(1)} %get-tuple-element.1353), channel_id=1, source_target_pairs={{16,0},{32,16},{48,32},{64,48},{80,64},{96,80},{112,96},{17,1},{33... | collective-permute-start | bytes 1572872 | tf_op jit(solution)/shard_map/ppermute | solution.py:37
  415.3 21.9 %collective-permute-start.10 = (f32[2,2,512,128]{3,2,1,0:T(8,128)}, f32[2,2,512,128]{3,2,1,0:T(8,128)}, u32[]{:S(2)}, u32[]{:S(2)}) collective-permute-start(f32[2,2,512,128]{3,2,1,0:T(8,128)} %get-tuple-element.1344), channel_id=1, source_target_pairs={{0,1},{1,2},{2,3},{3,4},{4,5},{5,6},{6,7},{7,8},{8,9},{9,10},{10,1... | collective-permute-start | bytes 3145736 | tf_op jit(solution)/shard_map/ppermute | solution.py:36
  425.1 16.4 %collective-permute-start.11 = (f32[2,2,512,128]{3,2,1,0:T(8,128)}, f32[2,2,512,128]{3,2,1,0:T(8,128)}, u32[]{:S(2)}, u32[]{:S(2)}) collective-permute-start(f32[2,2,512,128]{3,2,1,0:T(8,128)} %get-tuple-element.1345), channel_id=1, source_target_pairs={{1,0},{2,1},{3,2},{4,3},{5,4},{6,5},{7,6},{8,7},{9,8},{10,9},{11,1... | collective-permute-start | bytes 3145736 | tf_op jit(solution)/shard_map/ppermute | solution.py:37
  726.9 14.1 %collective-permute-start.12 = (f32[2,2,512,128]{3,2,1,0:T(8,128)}, f32[2,2,512,128]{3,2,1,0:T(8,128)}, u32[]{:S(2)}, u32[]{:S(2)}) collective-permute-start(f32[2,2,512,128]{3,2,1,0:T(8,128)} %get-tuple-element.1339), channel_id=1, source_target_pairs={{0,1},{1,2},{2,3},{3,4},{4,5},{5,6},{6,7},{7,8},{8,9},{9,10},{10,1... | collective-permute-start | bytes 3145736 | tf_op jit(solution)/shard_map/ppermute | solution.py:26
  729.0 16.4 %collective-permute-start.13 = (f32[2,2,512,128]{3,2,1,0:T(8,128)}, f32[2,2,512,128]{3,2,1,0:T(8,128)}, u32[]{:S(2)}, u32[]{:S(2)}) collective-permute-start(f32[2,2,512,128]{3,2,1,0:T(8,128)} %get-tuple-element.1338), channel_id=1, source_target_pairs={{1,0},{2,1},{3,2},{4,3},{5,4},{6,5},{7,6},{8,7},{9,8},{10,9},{11,1... | collective-permute-start | bytes 3145736 | tf_op jit(solution)/shard_map/ppermute | solution.py:26
  740.7 215.7 %all-reduce.3.cloned.1.call-start = ((), (), s32[]{:S(2)}) async-start(), calls=%async_computation | async-start | bytes 2097152 | tf_op jit(solution)/shard_map/psum | solution.py:16
  746.9 87.6 %copy-start.4 = (f32[2,2,256,256]{3,2,1,0:T(8,128)S(1)}, f32[2,2,256,256]{3,2,1,0:T(8,128)}, u32[]{:S(2)}) copy-start(f32[2,2,256,256]{3,2,1,0:T(8,128)} %copy-done.3) | copy-start | bytes 3145732
  748.0 84.1 %collective-permute-start.14 = (f32[2,2,128,256]{3,2,1,0:T(8,128)}, f32[2,2,128,256]{3,2,1,0:T(8,128)}, u32[]{:S(2)}, u32[]{:S(2)}) collective-permute-start(f32[2,2,128,256]{3,2,1,0:T(8,128)} %get-tuple-element.1343), channel_id=1, source_target_pairs={{0,16},{16,32},{32,48},{48,64},{64,80},{80,96},{96,112},{1,17},{17... | collective-permute-start | bytes 1572872 | tf_op jit(solution)/shard_map/ppermute | solution.py:26
  754.2 79.1 %collective-permute-start.15 = (f32[2,2,128,256]{3,2,1,0:T(8,128)}, f32[2,2,128,256]{3,2,1,0:T(8,128)}, u32[]{:S(2)}, u32[]{:S(2)}) collective-permute-start(f32[2,2,128,256]{3,2,1,0:T(8,128)} %get-tuple-element.1342), channel_id=1, source_target_pairs={{16,0},{32,16},{48,32},{64,48},{80,64},{96,80},{112,96},{17,1},{33... | collective-permute-start | bytes 1572872 | tf_op jit(solution)/shard_map/ppermute | solution.py:26
  833.3 123.1 %copy-start.10 = (f32[2,2,256,256]{3,2,1,0:T(8,128)S(1)}, f32[2,2,256,256]{3,2,1,0:T(8,128)}, u32[]{:S(2)}) copy-start(f32[2,2,256,256]{3,2,1,0:T(8,128)} %param.26) | copy-start | bytes 3145732
  (19 other events, 227.4 us)
Sparse Core Ops, SparseCore 0:
  740.8 91.2 all-reduce.4
  834.5 121.8 all-reduce.2
